TPU v7x, 32 devices: a whole 2x2x4 slice. The times are simulated.
32 devices in a mesh: dp: 2 (over core), shard: 16 (over z, y, x).
Axes of the slice: x: 2, y: 2, z: 4, core: 2. Of those that a mesh axis runs over, the one named last changes fastest.
Arguments:
- hidden_in: bfloat16 [4096, 1024], P(('dp', 'shard')), may hold values from -6 to 6
- doc_ids: int32 [32, 128], P(('dp', 'shard')), may hold values from 0 to 3, never falling along the last dimension, each value on 1 to 64 neighbouring positions
- expert_ids: int32 [4096], P(('dp', 'shard')), may hold values from 0 to 1, as said below
- slot_ids: int32 [4096], P(('dp', 'shard')), may hold values from 0 to 73, as said below
- out_grad: bfloat16 [4096, 1024], P(('dp', 'shard')), may hold values from -6 to 6
- ln1_gain: bfloat16 [1024], P(('dp', 'shard')), may hold values from 0.5 to 1.5
- ln1_bias: bfloat16 [1024], P(('dp', 'shard')), may hold values from -1 to 1
- w_query: bfloat16 [1024, 1024], P(('dp', 'shard')), may hold values from -0.1875 to 0.1875
- w_key: bfloat16 [1024, 1024], P(('dp', 'shard')), may hold values from -0.1875 to 0.1875
- w_value: bfloat16 [1024, 1024], P(('dp', 'shard')), may hold values from -0.1875 to 0.1875
- w_out: bfloat16 [1024, 1024], P(('dp', 'shard')), may hold values from -0.5 to 0.5
- ln2_gain: bfloat16 [1024], P(('dp', 'shard')), may hold values from 0.5 to 1.5
- ln2_bias: bfloat16 [1024], P(('dp', 'shard')), may hold values from -1 to 1
- w_up: bfloat16 [1024, 4096], P(('dp', 'shard')), may hold values from -0.1875 to 0.1875
- w_down: bfloat16 [4096, 1024], P(('dp', 'shard')), may hold values from -0.09375 to 0.09375
- w_router: bfloat16 [1024, 2], P(('dp', 'shard')), may hold values from -0.125 to 0.125
- w_mix: bfloat16 [1024, 2], P(('dp', 'shard')), may hold values from -0.1875 to 0.1875
- expert_up: bfloat16 [2, 1024, 4096], P(None, ('dp', 'shard')), may hold values from -0.1875 to 0.1875
- expert_down: bfloat16 [2, 4096, 1024], P(None, ('dp', 'shard')), may hold values from -0.09375 to 0.09375
- load_avg: float32 [2], replicated, may hold values from 0.05 to 0.3
Outputs:
- layer_out: bfloat16 [4096, 1024], P(('dp', 'shard'))
- input_grad: bfloat16 [4096, 1024], P(('dp', 'shard'))
- grad_ln1_gain: float32 [1024], P(('dp', 'shard'))
- grad_ln1_bias: float32 [1024], P(('dp', 'shard'))
- grad_w_query: float32 [1024, 1024], P(('dp', 'shard'))
- grad_w_key: float32 [1024, 1024], P(('dp', 'shard'))
- grad_w_value: float32 [1024, 1024], P(('dp', 'shard'))
- grad_w_out: float32 [1024, 1024], P(('dp', 'shard'))
- grad_ln2_gain: float32 [1024], P(('dp', 'shard'))
- grad_ln2_bias: float32 [1024], P(('dp', 'shard'))
- grad_w_up: float32 [1024, 4096], P(('dp', 'shard'))
- grad_w_down: float32 [4096, 1024], P(('dp', 'shard'))
- grad_w_router: float32 [1024, 2], P(('dp', 'shard'))
- grad_w_mix: float32 [1024, 2], P(('dp', 'shard'))
- grad_expert_up: float32 [2, 1024, 4096], P(None, ('dp', 'shard'))
- grad_expert_down: float32 [2, 4096, 1024], P(None, ('dp', 'shard'))
- expert_counts: int32 [2], replicated
- load_avg_new: float32 [2], replicated
Inputs may be any that keep to these rules, and one draw needn't show every extreme that they name: `expert_ids`: of the 128 tokens of one sequence at most 74 go to one expert, and in some sequence exactly 74 do. `slot_ids`: A token's slot is the number of earlier tokens of the same sequence routed to the same expert.
All inputs are finite; a program needn't handle non-finite values.
Results may differ from a plain program's by a relative error of at most 0.012.
The roundings to bfloat16 on the way count: a program that leaves them out, or rounds other values in their place, can miss the bound.
Values may be sent and summed in bfloat16 or wider, within the bound.
A program may use at most 384 MiB of HBM per device.

v0:
```python
import jax
import jax.numpy as jnp
from jax import lax
from jax.sharding import PartitionSpec as P

HEADS = 16
CAP = 74
BF = jnp.bfloat16
F32 = jnp.float32
BOTH = ("dp", "shard")


def mm(a, b, dims=((1,), (0,))):
    return lax.dot_general(a, b, (dims, ((), ())), preferred_element_type=F32)


def layer_norm(values, gain, bias):
    centre = values - jnp.mean(values, axis=-1, keepdims=True)
    scale_inv = lax.rsqrt(jnp.mean(centre * centre, axis=-1, keepdims=True) + 1e-05)
    normed = centre * scale_inv
    return (normed * gain + bias, normed, scale_inv)


def norm_back(grad_out, normed, scale_inv, gain):
    grad_normed = grad_out * gain
    inner = grad_normed - jnp.mean(grad_normed, axis=-1, keepdims=True)
    inner = inner - normed * jnp.mean(grad_normed * normed, axis=-1, keepdims=True)
    return (scale_inv * inner, jnp.sum(grad_out * normed, axis=0), jnp.sum(grad_out, axis=0))


def gelu_pair(t):
    inner = 0.7978845608 * (t + 0.044715 * t * t * t)
    th = jnp.tanh(inner)
    val = 0.5 * t * (1.0 + th)
    der = 0.5 * (1.0 + th) + 0.5 * t * (1.0 - th * th) * 0.7978845608 * (
        1.0 + 3.0 * 0.044715 * t * t
    )
    return (val, der)


def ag(block):
    return lax.all_gather(block, "shard", axis=0, tiled=False)


def rs(parts):
    return lax.psum_scatter(parts.astype(BF), "shard", scatter_dimension=0, tiled=False).astype(F32)


def body(
    hidden_in,
    doc_ids,
    expert_ids,
    slot_ids,
    out_grad,
    ln1_gain,
    ln1_bias,
    w_query,
    w_key,
    w_value,
    w_out,
    ln2_gain,
    ln2_bias,
    w_up,
    w_down,
    w_router,
    w_mix,
    expert_up,
    expert_down,
    load_avg,
):
    T, D = hidden_in.shape
    H, HD = (HEADS, D // HEADS)
    S = lax.axis_size("shard")
    C = lax.axis_size("dp")
    WR = w_query.shape[0]
    FF = w_up.shape[1]
    FR = w_down.shape[0]
    F = FR * C
    E = expert_up.shape[0]
    LO, HI = (80, T - 80)
    pos = jnp.where(
        expert_ids == 0, slot_ids, jnp.sum((expert_ids == 0).astype(jnp.int32)) + slot_ids
    )
    n0 = jnp.sum((expert_ids == 0).astype(jnp.int32))
    place = lax.iota(jnp.int32, T)
    perm = (pos[None, :] == place[:, None]).astype(BF)
    xs = mm(perm, hidden_in)
    dys = mm(perm, out_grad).astype(BF)
    doc = doc_ids[0]
    allowed = (place[None, :] <= place[:, None]) & (doc[:, None] == doc[None, :])
    allowed = mm(mm(perm, allowed.astype(BF)).astype(BF), perm, ((1,), (1,))) > 0.5
    is0 = (place < n0)[:, None]
    small = jnp.stack(
        [
            ln1_gain,
            ln1_bias,
            ln2_gain,
            ln2_bias,
            w_router[:, 0],
            w_router[:, 1],
            w_mix[:, 0],
            w_mix[:, 1],
        ]
    ).astype(F32)
    small = lax.all_gather(small, BOTH, axis=1, tiled=True)
    g1, b1, g2, b2 = (small[0], small[1], small[2], small[3])
    wr, wm = (small[4:6], small[6:8])
    wa = jnp.stack([w_query, w_key, w_value, w_out])
    wa = lax.all_gather(wa, BOTH, axis=1, tiled=True)
    wq, wk, wv, wo = (wa[0], wa[1], wa[2], wa[3])
    ups = jnp.stack([w_up, expert_up[0], expert_up[1]])
    ups = ups.reshape(3, WR, C, S, FR).transpose(3, 0, 1, 2, 4).reshape(S, 3, WR, F)
    ups = lax.all_to_all(ups, "shard", 0, 0)
    ups = lax.all_gather(ups, "dp", axis=0)
    ups = ups.transpose(2, 0, 1, 3, 4).reshape(3, D, F)
    downs = jnp.stack([w_down, expert_down[0], expert_down[1]])
    downs = lax.all_gather(downs, "dp", axis=1, tiled=True)
    dy_all = ag(dys)
    n1, u1, i1 = layer_norm(xs, g1, b1)
    h1b = n1.astype(BF)
    q = (mm(h1b, wq) * 0.125).astype(BF).reshape(T, H, HD)
    k = mm(h1b, wk).astype(BF).reshape(T, H, HD)
    v = mm(h1b, wv).astype(BF).reshape(T, H, HD)
    s = jnp.einsum("ihd,jhd->hij", q, k, preferred_element_type=F32)
    s = jnp.where(allowed[None], s, -1e30)
    ex = jnp.exp(s - jnp.max(s, axis=-1, keepdims=True))
    p = ex / jnp.sum(ex, axis=-1, keepdims=True)
    pb = p.astype(BF)
    o = jnp.einsum("hij,jhd->ihd", pb, v, preferred_element_type=F32).reshape(T, D).astype(BF)
    x1 = xs + mm(o, wo)
    h2, u2, i2 = layer_norm(x1, g2, b2)
    h2b = h2.astype(BF)

    def two(w):
        return jnp.stack([jnp.sum(h2 * w[0], axis=-1), jnp.sum(h2 * w[1], axis=-1)], axis=-1)

    r = jax.nn.softmax(two(wr), axis=-1)
    c = jax.nn.softmax(two(wm), axis=-1)
    gate = jnp.where(is0, r[:, 0:1], r[:, 1:2])
    c0, c1 = (c[:, 0:1], c[:, 1:2])
    we = c0 * gate
    scal = jnp.concatenate([c1, jnp.where(is0, we, 0.0), jnp.where(is0, 0.0, we)], axis=1)
    h_all = ag(h2b)
    scal_all = ag(scal)

    def cut(a, e):
        return (a[:, :LO] if e == 1 else a[:, HI:]) if e else a

    partial_y = jnp.zeros((S, T, D), F32)
    partial_dh = jnp.zeros((S, T, D), F32)
    score = []
    gup, gdown = ([], [])
    for e in range(3):
        he = cut(h_all, e)
        dye = cut(dy_all, e).astype(F32)
        se = cut(scal_all, e)[:, :, e : e + 1]
        n = he.shape[1]
        hf = he.reshape(S * n, D)
        pre = mm(hf, ups[e])
        val, der = gelu_pair(pre)
        ub = val.astype(BF)
        m = mm(ub, downs[e]).reshape(S, n, D)
        dm = (dye * se).astype(BF).reshape(S * n, D)
        dg = (mm(dm, downs[e], ((1,), (1,))) * der).astype(BF)
        gdown.append(mm(ub, dm, ((0,), (0,))))
        gup.append(mm(hf, dg, ((0,), (0,))))
        dx = mm(dg, ups[e], ((1,), (1,))).reshape(S, n, D)
        y = m * se
        sc = jnp.sum(dye * m, axis=-1)
        pad = [(0, 0), (0, T - n) if e < 2 else (T - n, 0)]
        live = is0[None, :, 0]
        partial_y += jnp.pad(y, pad + [(0, 0)])
        partial_dh += jnp.pad(dx, pad + [(0, 0)])
        score.append(jnp.pad(sc, pad))
    yfull = rs(partial_y)
    dh2 = rs(partial_dh)
    sc = lax.psum_scatter(jnp.stack(score, axis=1), "shard", scatter_dimension=0, tiled=False)
    sm = sc[0][:, None]
    se = jnp.where(is0, sc[1][:, None], sc[2][:, None])
    dc0, dc1 = (gate * se, sm)
    tot = c0 * dc0 + c1 * dc1
    dcl0, dcl1 = (c0 * (dc0 - tot), c1 * (dc1 - tot))
    dgate = c0 * se
    dr0, dr1 = (jnp.where(is0, dgate, 0.0), jnp.where(is0, 0.0, dgate))
    tot = r[:, 0:1] * dr0 + r[:, 1:2] * dr1
    drl0, drl1 = (r[:, 0:1] * (dr0 - tot), r[:, 1:2] * (dr1 - tot))
    layer_out = (x1 + yfull).astype(BF)
    dh2 = dh2 + drl0 * wr[0] + drl1 * wr[1] + dcl0 * wm[0] + dcl1 * wm[1]
    gw = [jnp.sum(h2 * t, axis=0) for t in (drl0, drl1, dcl0, dcl1)]
    dx1, gg2, gb2 = norm_back(dh2, u2, i2, g2)
    dx1 = dx1 + dys.astype(F32)
    dab = dx1.astype(BF)
    gwo = mm(o, dab, ((0,), (0,)))
    do = mm(dab, wo, ((1,), (1,))).astype(BF).reshape(T, H, HD)
    dp = jnp.einsum("ihd,jhd->hij", do, v, preferred_element_type=F32)
    ds = (p * (dp - jnp.sum(p * dp, axis=-1, keepdims=True))).astype(BF)
    dq = jnp.einsum("hij,jhd->ihd", ds, k, preferred_element_type=F32).astype(BF)
    dq = (dq * BF(0.125)).reshape(T, D)
    dk = jnp.einsum("hij,ihd->jhd", ds, q, preferred_element_type=F32).astype(BF).reshape(T, D)
    dv = jnp.einsum("hij,ihd->jhd", pb, do, preferred_element_type=F32).astype(BF).reshape(T, D)
    dh1 = mm(dq, wq, ((1,), (1,))) + mm(dk, wk, ((1,), (1,))) + mm(dv, wv, ((1,), (1,)))
    ga = jnp.stack(
        [mm(h1b, dq, ((0,), (0,))), mm(h1b, dk, ((0,), (0,))), mm(h1b, dv, ((0,), (0,))), gwo]
    )
    dxn, gg1, gb1 = norm_back(dh1, u1, i1, g1)
    input_grad = (dx1 + dxn).astype(BF)
    layer_out = mm(perm, layer_out, ((0,), (0,))).astype(BF)
    input_grad = mm(perm, input_grad, ((0,), (0,))).astype(BF)
    smalls = lax.psum(jnp.stack([gg1, gb1, gg2, gb2] + gw), BOTH)
    mine = lax.dynamic_slice_in_dim(smalls, lax.axis_index(BOTH) * WR, WR, 1)
    ga = ga.reshape(4, C, S, WR, D).transpose(1, 2, 0, 3, 4)
    ga = lax.psum_scatter(ga.astype(BF), "dp", scatter_dimension=0, tiled=False)
    ga = lax.psum_scatter(ga, "shard", scatter_dimension=0, tiled=False).astype(F32)
    gdown = lax.psum_scatter(jnp.stack(gdown), "dp", scatter_dimension=1, tiled=True)
    gup = jnp.stack(gup).reshape(3, C, S, WR, F).transpose(1, 2, 0, 3, 4)
    gup = lax.psum_scatter(gup, "dp", scatter_dimension=0, tiled=False).astype(BF)
    gup = lax.all_to_all(gup, "shard", 0, 0).astype(F32)
    gup = gup.reshape(S, 3, WR, C, FR).transpose(1, 2, 3, 0, 4).reshape(3, WR, FF)
    counts = lax.psum(jnp.stack([n0, T - n0]), BOTH)
    load_new = 0.9 * load_avg + 0.1 * counts.astype(F32) * E / (T * C * S)
    return (
        layer_out,
        input_grad,
        mine[0],
        mine[1],
        ga[0],
        ga[1],
        ga[2],
        ga[3],
        mine[2],
        mine[3],
        gup[0],
        gdown[0],
        jnp.stack([mine[4], mine[5]], axis=1),
        jnp.stack([mine[6], mine[7]], axis=1),
        gup[1:],
        gdown[1:],
        counts,
        load_new,
    )


def solution(mesh):
    row, vec = (P(BOTH, None), P(BOTH))
    mid = P(None, BOTH, None)
    return jax.shard_map(
        body,
        mesh=mesh,
        in_specs=(
            row,
            row,
            vec,
            vec,
            row,
            vec,
            vec,
            row,
            row,
            row,
            row,
            vec,
            vec,
            row,
            row,
            row,
            row,
            mid,
            mid,
            P(),
        ),
        out_specs=(
            row,
            row,
            vec,
            vec,
            row,
            row,
            row,
            row,
            vec,
            vec,
            row,
            row,
            row,
            row,
            mid,
            mid,
            P(),
            P(),
        ),
        check_vma=False,
    )
```

profile of v0, /device:TPU:0, one launch (start us, length us, event | category | flops | bytes accessed | tf_op | source)
XLA Modules:
  0.0 906.7 jit_solution(14686394213423674145)
XLA Ops:
  13.6 8.3 all-to-all-start
  22.1 81.6 %all-gather.4 = f32[32,32,8]{1,2,0:T(8,128)S(1)} all-gather(f32[1,32,8]{1,2,0:T(8,128)S(1)} %convert_bitcast_fusion.4), channel_id=1, replica_groups=mesh['dp'=2,'shard'=16] {'dp','shard'}, dimensions={0}, use_global_device_ids=true | all-gather | bytes 33792 | tf_op jit(solution)/shard_map/all_gather | solution.py:105
  125.9 70.1 %all-gather.15.cloned.1.call-done = bf16[2048,1024]{1,0:T(8,128)(2,1)} async-done(((bf16[128,1024]{1,0:T(8,128)(2,1)}), bf16[2048,1024]{1,0:T(8,128)(2,1)}) %all-gather.15.cloned.1.call-update) | async-done | bytes 4194320 | tf_op jit(solution)/shard_map/all_gather | solution.py:42
  205.8 4.4 fusion.52
  210.2 76.1 %all-gather.19.cloned.1.call-done = bf16[2048,1024]{1,0:T(8,128)(2,1)} async-done(((bf16[128,1024]{1,0:T(8,128)(2,1)}), bf16[2048,1024]{1,0:T(8,128)(2,1)}) %all-gather.19.cloned.1.call-update) | async-done | bytes 4194320 | tf_op jit(solution)/shard_map/all_gather | solution.py:42
  286.3 8.0 fusion.4
  297.4 6.0 fusion.2
  303.4 74.4 %all-reduce.6 = f32[16,3,128]{2,1,0:T(4,128)S(1)} all-reduce(f32[16,3,128]{2,1,0:T(4,128)S(1)} %pad_maximum_fusion.3), channel_id=8, replica_groups=mesh['dp'=2,'shard'=16] {'shard'}, use_global_device_ids=true, to_apply=%region_18.19.clone | all-reduce | flops 6144 | bytes 49152
  380.5 35.8 %all-gather.2 = f32[2048,3]{0,1:T(4,128)S(1)} all-gather(f32[128,3]{0,1:T(4,128)S(1)} %pad_maximum_fusion.4), channel_id=4, replica_groups=mesh['dp'=2,'shard'=16] {'shard'}, dimensions={0}, use_global_device_ids=true | all-gather | bytes 26112 | tf_op jit(solution)/shard_map/all_gather | solution.py:42
  416.4 10.2 %fusion.3 = (bf16[16,80,1024]{2,1,0:T(8,128)(2,1)S(1)}, bf16[16,80,1024]{2,1,0:T(8,128)(2,1)S(1)}, f32[16,80,1024]{2,1,0:T(8,128)}, f32[16,80,1024]{2,1,0:T(8,128)}) fusion(f32[16,80]{1,0:T(8,128)S(1)} %get-tuple-element.62, bf16[16,128,1024]{2,1,0:T(8,128)(2,1)} %bitcast.390, f32[16,80]{1,0:T(8,128)S(1)} %get-tuple-element.63, f32[16,80,1024]{2,1,0:T(8,128)} %fusion.52, ...), kind=kLoop, calls=%fused_computation.12 | loop fusion | flops 10485760 | bytes 31467520 | tf_op jit(solution)/shard_map/convert_element_type | solution.py:163
  432.7 3.5 fusion.120
  438.2 7.0 fusion.1
  445.2 5.2 fusion.7
  454.9 92.5 %reduce-scatter.15.cloned.1.call-done = bf16[1,128,1024]{2,1,0:T(8,128)(2,1)} async-done(((bf16[16,128,1024]{2,1,0:T(8,128)(2,1)}), bf16[1,128,1024]{2,1,0:T(8,128)(2,1)}) %reduce-scatter.15.cloned.1.call-update) | async-done | bytes 262160 | tf_op jit(solution)/shard_map/reduce_scatter | solution.py:46
  560.0 3.8 maximum_bitcast_fusion
  574.0 4.6 copy.102
  578.7 4.4 copy.103
  583.1 6.6 copy.101
  599.3 12.2 %all-reduce.17 = bf16[2,16,3,32,256]{4,3,1,0,2:T(8,128)(2,1)S(1)} all-reduce(f32[2,16,3,32,256]{4,3,1,0,2:T(8,128)} %maximum_bitcast_fusion.1), channel_id=11, replica_groups=mesh['dp'=2,'shard'=16] {'dp'}, use_global_device_ids=true, to_apply=%region_35.36.clone | all-reduce | flops 786432 | bytes 4718592
  613.2 5.7 all-to-all-start.1
  619.0 5.6 dynamic-slice_bitcast_fusion
  626.0 48.3 %psum.15 = s32[2]{0:T(128)S(1)} all-reduce(s32[2]{0:T(128)S(1)} %pad_add_fusion), channel_id=1, replica_groups=mesh['dp'=2,'shard'=16] {'dp','shard'}, use_global_device_ids=true, to_apply=%region_37.38 | all-reduce | flops 2 | bytes 16 | tf_op jit(solution)/shard_map/psum | solution.py:219
  692.7 43.1 %psum.14 = f32[8,1024]{1,0:T(8,128)S(1)} all-reduce(f32[8,1024]{1,0:T(8,128)S(1)} %stack.176), channel_id=1, replica_groups=mesh['dp'=2,'shard'=16] {'dp','shard'}, use_global_device_ids=true, to_apply=%region_32.33 | all-reduce | flops 8192 | bytes 65536 | tf_op jit(solution)/shard_map/psum | solution.py:209
  740.6 156.4 %all-reduce.16.cloned.1.call-done = bf16[16,4,32,1024]{3,2,0,1:T(8,128)(2,1)} async-done(((bf16[16,4,32,1024]{3,2,0,1:T(8,128)(2,1)}), bf16[16,4,32,1024]{3,2,0,1:T(8,128)(2,1)}) %all-reduce.16.cloned.1.call-update) | async-done | bytes 4194320
  (279 shorter events, 116.4 us)
Async XLA Ops:
  7.2 98.4 %copy-start = (bf16[128,1024]{1,0:T(8,128)(2,1)S(1)}, bf16[128,1024]{1,0:T(8,128)(2,1)}, u32[]{:S(2)}) copy-start(bf16[128,1024]{1,0:T(8,128)(2,1)} %param.20) | copy-start | bytes 786436
  7.2 100.0 %all-gather.11.cloned.1.call-start = ((), (), s32[]{:S(2)}) async-start(), calls=%async_computation.5 | async-start | bytes 8650752 | tf_op jit(solution)/shard_map/all_gather | solution.py:109
  11.1 10.9 %copy-start.45 = (bf16[32,2]{0,1:T(2,128)(2,1)S(1)}, bf16[32,2]{0,1:T(2,128)(2,1)}, u32[]{:S(2)}) copy-start(bf16[32,2]{0,1:T(2,128)(2,1)} %param.35) | copy-start | bytes 388
  11.1 10.9 %copy-start.46 = (bf16[32]{0:T(256)(128)(2,1)S(1)}, bf16[32]{0:T(256)(128)(2,1)}, u32[]{:S(2)}) copy-start(bf16[32]{0:T(256)(128)(2,1)} %param.25) | copy-start | bytes 196
  11.1 10.9 %copy-start.47 = (bf16[32]{0:T(256)(128)(2,1)S(1)}, bf16[32]{0:T(256)(128)(2,1)}, u32[]{:S(2)}) copy-start(bf16[32]{0:T(256)(128)(2,1)} %param.26) | copy-start | bytes 196
  11.1 10.9 %copy-start.48 = (bf16[32]{0:T(256)(128)(2,1)S(1)}, bf16[32]{0:T(256)(128)(2,1)}, u32[]{:S(2)}) copy-start(bf16[32]{0:T(256)(128)(2,1)} %param.31) | copy-start | bytes 196
  11.1 10.9 %copy-start.49 = (bf16[32]{0:T(256)(128)(2,1)S(1)}, bf16[32]{0:T(256)(128)(2,1)}, u32[]{:S(2)}) copy-start(bf16[32]{0:T(256)(128)(2,1)} %param.32) | copy-start | bytes 196
  12.1 91.7 %copy-start.51 = (s32[128]{0:T(128)S(1)}, s32[128]{0:T(128)}, u32[]{:S(2)}) copy-start(s32[128]{0:T(128)} %param.22) | copy-start | bytes 1540
  12.2 92.3 %copy-start.50 = (s32[128]{0:T(128)S(1)}, s32[128]{0:T(128)}, u32[]{:S(2)}) copy-start(s32[128]{0:T(128)} %param.23) | copy-start | bytes 1540
  12.2 93.0 %copy-start.52 = (s32[1,128]{1,0:T(1,128)S(1)}, s32[1,128]{1,0:T(1,128)}, u32[]{:S(2)}) copy-start(s32[1,128]{1,0:T(1,128)} %param.21) | copy-start | bytes 1540
  13.6 92.6 %all-to-all-start = ((bf16[16,3,32,256]{3,2,1,0:T(8,128)(2,1)}), bf16[16,3,32,256]{3,2,1,0:T(8,128)(2,1)S(1)}, u32[]{:S(2)}, u32[]{:S(2)}) async-start(bf16[16,3,32,256]{3,2,1,0:T(8,128)(2,1)} %reshape.288), calls=%async_computation | async-start | bytes 1572864 | tf_op jit(solution)/shard_map/all_to_all | solution.py:113
  21.9 101.5 %all-gather.17.cloned.1.call-start = ((), (), s32[]{:S(2)}) async-start(), calls=%async_computation.11 | async-start | bytes 2359296 | tf_op jit(solution)/shard_map/all_gather | solution.py:114
  107.1 88.9 %all-gather.15.cloned.1.call-start = ((), (), s32[]{:S(2)}) async-start(), calls=%async_computation.10 | async-start | bytes 4456448 | tf_op jit(solution)/shard_map/all_gather | solution.py:42
  120.1 85.7 %all-gather.13.cloned.1.call-start = ((), (), s32[]{:S(2)}) async-start(), calls=%async_computation.6 | async-start | bytes 2359296 | tf_op jit(solution)/shard_map/all_gather | solution.py:117
  121.2 165.1 %all-gather.19.cloned.1.call-start = ((), (), s32[]{:S(2)}) async-start(), calls=%async_computation.12 | async-start | bytes 4456448 | tf_op jit(solution)/shard_map/all_gather | solution.py:42
  122.2 425.2 %reduce-scatter.15.cloned.1.call-start = ((), (), s32[]{:S(2)}) async-start(), calls=%async_computation.8 | async-start | bytes 4456448 | tf_op jit(solution)/shard_map/reduce_scatter | solution.py:46
  454.3 94.8 %copy-start.14 = (bf16[128,1024]{1,0:T(8,128)(2,1)S(1)}, bf16[128,1024]{1,0:T(8,128)(2,1)}, u32[]{:S(2)}) copy-start(bf16[128,1024]{1,0:T(8,128)(2,1)} %convolution_convert_fusion.4) | copy-start | bytes 786436
  454.3 164.6 %all-reduce.14.cloned.1.call-start = ((), (), s32[]{:S(2)}) async-start(), calls=%async_computation.13 | async-start | bytes 16777216
  563.9 116.9 %reduce-scatter.17.cloned.1.call-start = ((), (), s32[]{:S(2)}) async-start(), calls=%async_computation.9 | async-start | bytes 4718592 | tf_op jit(solution)/shard_map/reduce_scatter | solution.py:214
  572.5 165.1 %reduce-scatter.13.cloned.1.call-start = ((), (), s32[]{:S(2)}) async-start(), calls=%async_computation.7 | async-start | bytes 4456448 | tf_op jit(solution)/shard_map/reduce_scatter | solution.py:46
  613.2 61.6 %all-to-all-start.1 = ((bf16[16,3,32,256]{3,2,1,0:T(8,128)(2,1)}), bf16[16,3,32,256]{3,2,1,0:T(8,128)(2,1)}, u32[]{:S(2)}, u32[]{:S(2)}) async-start(bf16[16,3,32,256]{3,2,1,0:T(8,128)(2,1)} %copy.104), calls=%async_computation.3 | async-start | bytes 1572864 | tf_op jit(solution)/shard_map/all_to_all | solution.py:217
  618.9 278.1 %all-reduce.16.cloned.1.call-start = ((), (), s32[]{:S(2)}) async-start(), calls=%async_computation.14 | async-start | bytes 8388608
  624.6 49.7 %copy-start.53 = (f32[2]{0:T(128)S(1)}, f32[2]{0:T(128)}, u32[]{:S(2)}) copy-start(f32[2]{0:T(128)} %param.39) | copy-start | bytes 28
  737.6 161.9 %copy-start.1 = (bf16[128,1024]{1,0:T(8,128)(2,1)S(1)}, bf16[128,1024]{1,0:T(8,128)(2,1)}, u32[]{:S(2)}) copy-start(bf16[128,1024]{1,0:T(8,128)(2,1)} %param.20) | copy-start | bytes 786436
  (53 other events, 196.3 us)
Sparse Core Ops, SparseCore 0:
  11.5 86.9 all-gather.10
  107.2 8.1 all-gather.16
  120.2 75.7 all-gather.14
  197.4 8.3 all-gather.12
  209.0 77.2 all-gather.18
  454.4 92.9 reduce-scatter.14
  564.0 38.4 all-reduce.13
  604.7 12.2 reduce-scatter.16
  619.4 101.9 reduce-scatter.12
  727.8 169.1 all-reduce.15
where the time goes:
time: 914 us; the launch traced here: 907 us
  waiting for transfers between devices  397 us (43%)
  blocking collectives  296 us (32%)
  matrix products  86.9 us (10%)
  local copies, waits for them, and re-layouts  55.6 us (6%)
  other arithmetic  40 us (4%)
  between operations  16.4 us (2%)
  starting transfers between devices  15.4 us (2%)
    unnamed x12, waiting for transfers between devices  157 us
    all_gather x2, waiting for transfers between devices, ag(): return lax.all_gather(block, 'shard', axis=0, tiled=False)  146 us
    reduce_scatter x2, waiting for transfers between devices, rs(): lax.psum_scatter(parts.astype(BF), 'shard', scatter_dimension=0, tiled=Fa...  92.5 us
    unnamed x2, blocking collectives  86.7 us
    all_gather x1, blocking collectives, body(): small = lax.all_gather(small, BOTH, axis=1, tiled=True)  81.6 us
    dot_general x35, matrix products, mm(): return lax.dot_general(a, b, (dims, ((), ())), preferred_element_type=F32)  80.9 us
    psum x1, blocking collectives, body(): counts = lax.psum(jnp.stack([n0, T - n0]), BOTH)  48.3 us
    psum x1, blocking collectives, body(): smalls = lax.psum(jnp.stack([gg1, gb1, gg2, gb2] + gw), BOTH)  43.1 us
  transfers between devices with their start and end apart: 12, of which 5 were waited for; matrix products, arithmetic and copies ran while one was open for 11% of the time, Pallas kernels for 0%

commit v1 on v0

--- a/solution.py
+++ b/solution.py
@@ -8,6 +8,12 @@
 BF = jnp.bfloat16
 F32 = jnp.float32
 BOTH = ("dp", "shard")
+
+
+def reach_results_all(inp):
+    for dd in ("shard", "dp"):
+        inp = lax.psum(inp, axis_name=dd)
+    return inp
 
 
 def mm(a, b, dims=((1,), (0,))):
@@ -216,7 +222,7 @@
     gup = lax.psum_scatter(gup, "dp", scatter_dimension=0, tiled=False).astype(BF)
     gup = lax.all_to_all(gup, "shard", 0, 0).astype(F32)
     gup = gup.reshape(S, 3, WR, C, FR).transpose(1, 2, 3, 0, 4).reshape(3, WR, FF)
-    counts = lax.psum(jnp.stack([n0, T - n0]), BOTH)
+    counts = reach_results_all(jnp.stack([n0, T - n0]))
     load_new = 0.9 * load_avg + 0.1 * counts.astype(F32) * E / (T * C * S)
     return (
         layer_out,

time: 914 us -> 913 us (level)
  blocking collectives: 296 us -> 269 us
  waiting for transfers between devices: 397 us -> 423 us
    psum x1 -> x2, blocking collectives: 48.3 us -> 20.6 us  [reach_results_all(): inp = lax.psum(inp, axis_name=dd)]
    unnamed x12, waiting for transfers between devices: 157 us -> 173 us
    reduce_scatter x2, waiting for transfers between devices: 92.5 us -> 102 us  [rs(): lax.psum_scatter(parts.astype(BF), 'shard', scatter_dimension=0, tiled=Fa...]
  transfers between devices with their start and end apart: 12 -> 12, of which waited for: 5 -> 6; matrix products, arithmetic and copies ran while one was open for 11% -> 11% of each run, Pallas kernels for 0% -> 0%
where the time goes in v1:
time: 913 us; the launch traced here: 906 us
  waiting for transfers between devices  423 us (46%)
  blocking collectives  269 us (29%)
  matrix products  86.9 us (10%)
  local copies, waits for them, and re-layouts  55.4 us (6%)
  other arithmetic  40 us (4%)
  between operations  16.4 us (2%)
  starting transfers between devices  15.5 us (2%)
    unnamed x12, waiting for transfers between devices  173 us
    all_gather x2, waiting for transfers between devices, ag(): return lax.all_gather(block, 'shard', axis=0, tiled=False)  146 us
    reduce_scatter x2, waiting for transfers between devices, rs(): lax.psum_scatter(parts.astype(BF), 'shard', scatter_dimension=0, tiled=Fa...  102 us
    unnamed x2, blocking collectives  86.7 us
    all_gather x1, blocking collectives, body(): small = lax.all_gather(small, BOTH, axis=1, tiled=True)  81.6 us
    dot_general x35, matrix products, mm(): return lax.dot_general(a, b, (dims, ((), ())), preferred_element_type=F32)  80.9 us
    psum x1, blocking collectives, body(): smalls = lax.psum(jnp.stack([gg1, gb1, gg2, gb2] + gw), BOTH)  44.2 us
    all_gather x1, blocking collectives, ag(): return lax.all_gather(block, 'shard', axis=0, tiled=False)  35.8 us
  transfers between devices with their start and end apart: 12, of which 6 were waited for; matrix products, arithmetic and copies ran while one was open for 11% of the time, Pallas kernels for 0%

profile of v1, /device:TPU:0, one launch (start us, length us, event | category | flops | bytes accessed | tf_op | source)
XLA Modules:
  0.0 906.3 jit_solution(8733417576058844713)
XLA Ops:
  13.6 8.3 all-to-all-start
  22.1 81.6 %all-gather.4 = f32[32,32,8]{1,2,0:T(8,128)S(1)} all-gather(f32[1,32,8]{1,2,0:T(8,128)S(1)} %convert_bitcast_fusion.4), channel_id=1, replica_groups=mesh['dp'=2,'shard'=16] {'dp','shard'}, dimensions={0}, use_global_device_ids=true | all-gather | bytes 33792 | tf_op jit(solution)/shard_map/all_gather | solution.py:111
  125.9 70.1 %all-gather.15.cloned.1.call-done = bf16[2048,1024]{1,0:T(8,128)(2,1)} async-done(((bf16[128,1024]{1,0:T(8,128)(2,1)}), bf16[2048,1024]{1,0:T(8,128)(2,1)}) %all-gather.15.cloned.1.call-update) | async-done | bytes 4194320 | tf_op jit(solution)/shard_map/all_gather | solution.py:48
  205.8 4.4 fusion.52
  210.2 76.1 %all-gather.19.cloned.1.call-done = bf16[2048,1024]{1,0:T(8,128)(2,1)} async-done(((bf16[128,1024]{1,0:T(8,128)(2,1)}), bf16[2048,1024]{1,0:T(8,128)(2,1)}) %all-gather.19.cloned.1.call-update) | async-done | bytes 4194320 | tf_op jit(solution)/shard_map/all_gather | solution.py:48
  286.3 8.0 fusion.4
  297.4 6.0 fusion.2
  303.4 74.4 %all-reduce.6 = f32[16,3,128]{2,1,0:T(4,128)S(1)} all-reduce(f32[16,3,128]{2,1,0:T(4,128)S(1)} %pad_maximum_fusion.3), channel_id=8, replica_groups=mesh['dp'=2,'shard'=16] {'shard'}, use_global_device_ids=true, to_apply=%region_18.19.clone | all-reduce | flops 6144 | bytes 49152
  380.5 35.8 %all-gather.2 = f32[2048,3]{0,1:T(4,128)S(1)} all-gather(f32[128,3]{0,1:T(4,128)S(1)} %pad_maximum_fusion.4), channel_id=4, replica_groups=mesh['dp'=2,'shard'=16] {'shard'}, dimensions={0}, use_global_device_ids=true | all-gather | bytes 26112 | tf_op jit(solution)/shard_map/all_gather | solution.py:48
  416.4 10.2 %fusion.3 = (bf16[16,80,1024]{2,1,0:T(8,128)(2,1)S(1)}, bf16[16,80,1024]{2,1,0:T(8,128)(2,1)S(1)}, f32[16,80,1024]{2,1,0:T(8,128)}, f32[16,80,1024]{2,1,0:T(8,128)}) fusion(f32[16,80]{1,0:T(8,128)S(1)} %get-tuple-element.62, bf16[16,128,1024]{2,1,0:T(8,128)(2,1)} %bitcast.390, f32[16,80]{1,0:T(8,128)S(1)} %get-tuple-element.63, f32[16,80,1024]{2,1,0:T(8,128)} %fusion.52, ...), kind=kLoop, calls=%fused_computation.12 | loop fusion | flops 10485760 | bytes 31467520 | tf_op jit(solution)/shard_map/convert_element_type | solution.py:169
  438.2 7.0 fusion.1
  445.2 5.2 fusion.7
  455.0 92.5 %reduce-scatter.15.cloned.1.call-done = bf16[1,128,1024]{2,1,0:T(8,128)(2,1)} async-done(((bf16[16,128,1024]{2,1,0:T(8,128)(2,1)}), bf16[1,128,1024]{2,1,0:T(8,128)(2,1)}) %reduce-scatter.15.cloned.1.call-update) | async-done | bytes 262160 | tf_op jit(solution)/shard_map/reduce_scatter | solution.py:52
  560.1 3.8 maximum_bitcast_fusion
  574.1 4.6 copy.102
  578.7 4.4 copy.103
  583.1 6.5 copy.101
  599.2 12.2 %all-reduce.17 = bf16[2,16,3,32,256]{4,3,1,0,2:T(8,128)(2,1)S(1)} all-reduce(f32[2,16,3,32,256]{4,3,1,0,2:T(8,128)} %maximum_bitcast_fusion.1), channel_id=11, replica_groups=mesh['dp'=2,'shard'=16] {'dp'}, use_global_device_ids=true, to_apply=%region_35.36.clone | all-reduce | flops 786432 | bytes 4718592
  613.1 5.8 all-to-all-start.1
  619.0 5.6 dynamic-slice_bitcast_fusion
  626.0 18.8 %psum.22 = s32[2]{0:T(128)S(1)} all-reduce(s32[2]{0:T(128)S(1)} %pad_add_fusion), channel_id=1, replica_groups=mesh['dp'=2,'shard'=16] {'shard'}, use_global_device_ids=true, to_apply=%region_37.38 | all-reduce | flops 2 | bytes 16 | tf_op jit(solution)/shard_map/psum | solution.py:15
  665.0 44.2 %psum.21 = f32[8,1024]{1,0:T(8,128)S(1)} all-reduce(f32[8,1024]{1,0:T(8,128)S(1)} %stack.176), channel_id=1, replica_groups=mesh['dp'=2,'shard'=16] {'dp','shard'}, use_global_device_ids=true, to_apply=%region_32.33 | all-reduce | flops 8192 | bytes 65536 | tf_op jit(solution)/shard_map/psum | solution.py:215
  711.0 9.9 %reduce-scatter.13.cloned.1.call-done = bf16[1,128,1024]{2,1,0:T(8,128)(2,1)} async-done(((bf16[16,128,1024]{2,1,0:T(8,128)(2,1)}), bf16[1,128,1024]{2,1,0:T(8,128)(2,1)}) %reduce-scatter.13.cloned.1.call-update) | async-done | bytes 262160 | tf_op jit(solution)/shard_map/reduce_scatter | solution.py:52
  723.9 172.6 %all-reduce.16.cloned.1.call-done = bf16[16,4,32,1024]{3,2,0,1:T(8,128)(2,1)} async-done(((bf16[16,4,32,1024]{3,2,0,1:T(8,128)(2,1)}), bf16[16,4,32,1024]{3,2,0,1:T(8,128)(2,1)}) %all-reduce.16.cloned.1.call-update) | async-done | bytes 4194320
  (280 shorter events, 121.7 us)
Async XLA Ops:
  7.2 98.4 %copy-start = (bf16[128,1024]{1,0:T(8,128)(2,1)S(1)}, bf16[128,1024]{1,0:T(8,128)(2,1)}, u32[]{:S(2)}) copy-start(bf16[128,1024]{1,0:T(8,128)(2,1)} %param.20) | copy-start | bytes 786436
  7.2 100.0 %all-gather.11.cloned.1.call-start = ((), (), s32[]{:S(2)}) async-start(), calls=%async_computation.5 | async-start | bytes 8650752 | tf_op jit(solution)/shard_map/all_gather | solution.py:115
  11.1 10.9 %copy-start.45 = (bf16[32,2]{0,1:T(2,128)(2,1)S(1)}, bf16[32,2]{0,1:T(2,128)(2,1)}, u32[]{:S(2)}) copy-start(bf16[32,2]{0,1:T(2,128)(2,1)} %param.35) | copy-start | bytes 388
  11.1 10.9 %copy-start.46 = (bf16[32]{0:T(256)(128)(2,1)S(1)}, bf16[32]{0:T(256)(128)(2,1)}, u32[]{:S(2)}) copy-start(bf16[32]{0:T(256)(128)(2,1)} %param.25) | copy-start | bytes 196
  11.1 10.9 %copy-start.47 = (bf16[32]{0:T(256)(128)(2,1)S(1)}, bf16[32]{0:T(256)(128)(2,1)}, u32[]{:S(2)}) copy-start(bf16[32]{0:T(256)(128)(2,1)} %param.26) | copy-start | bytes 196
  11.1 10.9 %copy-start.48 = (bf16[32]{0:T(256)(128)(2,1)S(1)}, bf16[32]{0:T(256)(128)(2,1)}, u32[]{:S(2)}) copy-start(bf16[32]{0:T(256)(128)(2,1)} %param.31) | copy-start | bytes 196
  11.1 10.9 %copy-start.49 = (bf16[32]{0:T(256)(128)(2,1)S(1)}, bf16[32]{0:T(256)(128)(2,1)}, u32[]{:S(2)}) copy-start(bf16[32]{0:T(256)(128)(2,1)} %param.32) | copy-start | bytes 196
  12.1 91.7 %copy-start.51 = (s32[128]{0:T(128)S(1)}, s32[128]{0:T(128)}, u32[]{:S(2)}) copy-start(s32[128]{0:T(128)} %param.22) | copy-start | bytes 1540
  12.2 92.3 %copy-start.50 = (s32[128]{0:T(128)S(1)}, s32[128]{0:T(128)}, u32[]{:S(2)}) copy-start(s32[128]{0:T(128)} %param.23) | copy-start | bytes 1540
  12.2 93.0 %copy-start.52 = (s32[1,128]{1,0:T(1,128)S(1)}, s32[1,128]{1,0:T(1,128)}, u32[]{:S(2)}) copy-start(s32[1,128]{1,0:T(1,128)} %param.21) | copy-start | bytes 1540
  13.6 92.6 %all-to-all-start = ((bf16[16,3,32,256]{3,2,1,0:T(8,128)(2,1)}), bf16[16,3,32,256]{3,2,1,0:T(8,128)(2,1)S(1)}, u32[]{:S(2)}, u32[]{:S(2)}) async-start(bf16[16,3,32,256]{3,2,1,0:T(8,128)(2,1)} %reshape.288), calls=%async_computation | async-start | bytes 1572864 | tf_op jit(solution)/shard_map/all_to_all | solution.py:119
  21.9 101.5 %all-gather.17.cloned.1.call-start = ((), (), s32[]{:S(2)}) async-start(), calls=%async_computation.11 | async-start | bytes 2359296 | tf_op jit(solution)/shard_map/all_gather | solution.py:120
  107.1 88.9 %all-gather.15.cloned.1.call-start = ((), (), s32[]{:S(2)}) async-start(), calls=%async_computation.10 | async-start | bytes 4456448 | tf_op jit(solution)/shard_map/all_gather | solution.py:48
  120.1 85.7 %all-gather.13.cloned.1.call-start = ((), (), s32[]{:S(2)}) async-start(), calls=%async_computation.6 | async-start | bytes 2359296 | tf_op jit(solution)/shard_map/all_gather | solution.py:123
  121.2 165.1 %all-gather.19.cloned.1.call-start = ((), (), s32[]{:S(2)}) async-start(), calls=%async_computation.12 | async-start | bytes 4456448 | tf_op jit(solution)/shard_map/all_gather | solution.py:48
  122.2 425.2 %reduce-scatter.15.cloned.1.call-start = ((), (), s32[]{:S(2)}) async-start(), calls=%async_computation.8 | async-start | bytes 4456448 | tf_op jit(solution)/shard_map/reduce_scatter | solution.py:52
  454.4 94.8 %copy-start.14 = (bf16[128,1024]{1,0:T(8,128)(2,1)S(1)}, bf16[128,1024]{1,0:T(8,128)(2,1)}, u32[]{:S(2)}) copy-start(bf16[128,1024]{1,0:T(8,128)(2,1)} %convolution_convert_fusion.4) | copy-start | bytes 786436
  454.4 164.6 %all-reduce.14.cloned.1.call-start = ((), (), s32[]{:S(2)}) async-start(), calls=%async_computation.13 | async-start | bytes 16777216
  563.9 89.2 %reduce-scatter.17.cloned.1.call-start = ((), (), s32[]{:S(2)}) async-start(), calls=%async_computation.9 | async-start | bytes 4718592 | tf_op jit(solution)/shard_map/reduce_scatter | solution.py:220
  572.6 148.3 %reduce-scatter.13.cloned.1.call-start = ((), (), s32[]{:S(2)}) async-start(), calls=%async_computation.7 | async-start | bytes 4456448 | tf_op jit(solution)/shard_map/reduce_scatter | solution.py:52
  613.1 34.0 %all-to-all-start.1 = ((bf16[16,3,32,256]{3,2,1,0:T(8,128)(2,1)}), bf16[16,3,32,256]{3,2,1,0:T(8,128)(2,1)}, u32[]{:S(2)}, u32[]{:S(2)}) async-start(bf16[16,3,32,256]{3,2,1,0:T(8,128)(2,1)} %copy.104), calls=%async_computation.3 | async-start | bytes 1572864 | tf_op jit(solution)/shard_map/all_to_all | solution.py:223
  618.9 277.6 %all-reduce.16.cloned.1.call-start = ((), (), s32[]{:S(2)}) async-start(), calls=%async_computation.14 | async-start | bytes 8388608
  624.6 22.0 %copy-start.53 = (f32[2]{0:T(128)S(1)}, f32[2]{0:T(128)}, u32[]{:S(2)}) copy-start(f32[2]{0:T(128)} %param.39) | copy-start | bytes 28
  720.8 178.2 %copy-start.1 = (bf16[128,1024]{1,0:T(8,128)(2,1)S(1)}, bf16[128,1024]{1,0:T(8,128)(2,1)}, u32[]{:S(2)}) copy-start(bf16[128,1024]{1,0:T(8,128)(2,1)} %param.20) | copy-start | bytes 786436
  (53 other events, 196.3 us)
Sparse Core Ops, SparseCore 0:
  11.5 86.9 all-gather.10
  107.2 8.1 all-gather.16
  120.2 75.7 all-gather.14
  197.4 8.3 all-gather.12
  209.0 77.2 all-gather.18
  454.5 92.9 reduce-scatter.14
  564.0 38.4 all-reduce.13
  604.7 12.2 reduce-scatter.16
  619.5 101.3 reduce-scatter.12
  727.3 169.2 all-reduce.15
